TPU v7x, 128 devices: a whole 4x4x4 slice. The times are simulated.
128 devices in a mesh: row: 8 (over z, core), col: 16 (over x, y).
Axes of the slice: x: 4, y: 4, z: 4, core: 2. Of those that a mesh axis runs over, the one named last changes fastest.
Arguments:
- offsets: float32 [8, 16, 2, 256], P('row', 'col'), may hold values from 0 to 1
- point_order: int32 [8, 16, 256], P('row', 'col'), may hold values from 0 to 255, each once within a row
- nugget: float32 [8, 16, 256], P('row', 'col'), may hold values from 1 to 4
- interp: float32 [8, 16, 128, 128], P('row', 'col'), may hold values from -0.5 to 0.5
Outputs:
- root_work: float32 [16384, 16384], P('row', 'col')
Inputs may be any that keep to these rules, and one draw needn't show every extreme that they name: `point_order`: each row lists every point of its box once; its first 128 entries name the box's skeleton points.
All inputs are finite; a program needn't handle non-finite values.
Results may differ from a plain program's by a relative error of at most 0.0001.
Values sent between devices are 32-bit elements; how exact they have to be, the bound alone decides.
A program may use at most 128 MiB of HBM per device.

v0:
```python
import jax
import jax.numpy as jnp
from jax import lax
from jax.sharding import PartitionSpec as P

PW = 512
kernel_amp = 0.015625
kernel_len = 0.5
highest = lax.Precision.HIGHEST


def extended(block, sides, width):
    for axis, dim in sides:
        count = lax.axis_size(axis)
        forward = [(i, i + 1) for i in range(count - 1)]
        backward = [(target, source) for source, target in forward]
        low = lax.ppermute(
            lax.slice_in_dim(block, block.shape[dim] - width, None, axis=dim), axis, forward
        )
        high = lax.ppermute(lax.slice_in_dim(block, 0, width, axis=dim), axis, backward)
        block = jnp.concatenate([low, block, high], axis=dim)
    return block


def shifted(block, axis, distance):
    devices = range(lax.axis_size(axis))
    route = [(i - distance, i) for i in devices if i - distance in devices]
    return lax.ppermute(block, axis, route)


def spread_2(value, axis, source):
    kept = jnp.where(lax.axis_index(axis) == source, value, 0).astype(value.dtype)
    return lax.psum(kept, axis)


def offsets_all():
    return [(a, b) for a in (-1, 0, 1) for b in (-1, 0, 1)]


def pairs_all():
    return [
        (e, m)
        for e in offsets_all()
        for m in offsets_all()
        if abs(m[0] - e[0]) <= 1 and abs(m[1] - e[1]) <= 1
    ]


def block_of(a, b):
    return (a + 1) * 3 + (b + 1)


def vector(along, across):
    return (along, across)


def kernel(left, right):
    gap_row = left[0][:, None] - right[0][None, :]
    gap_col = left[1][:, None] - right[1][None, :]
    return kernel_amp * jnp.exp(-jnp.sqrt(gap_row * gap_row + gap_col * gap_col) / kernel_len)


def cross_pair(stored, target, columns):
    pair_index = {pair: n for n, pair in enumerate(pairs_all())}
    left_rows = []
    right_rows = []
    for e in offsets_all():
        if abs(target[0] - e[0]) <= 1 and abs(target[1] - e[1]) <= 1:
            left_rows.append(stored[pair_index[e, (0, 0)]][:, :columns])
            right_rows.append(stored[pair_index[e, target]][:, :columns])
    return (jnp.concatenate(left_rows, axis=0), jnp.concatenate(right_rows, axis=0))


def cross_sum(stored, target, columns):
    left_rows, right_rows = cross_pair(stored, target, columns)
    return jnp.einsum("rk,rl->kl", left_rows, right_rows, precision=highest)


def eliminate(stored, near_matrix, interp_box):
    box_points = near_matrix.shape[0]
    skel_count = interp_box.shape[0]
    fill_blocks = [cross_sum(stored, m, box_points) for m in offsets_all()]
    matrix = near_matrix - jnp.concatenate(fill_blocks, axis=1)
    reduced_rows = matrix[skel_count:] - jnp.einsum(
        "sr,sk->rk", interp_box, matrix[:skel_count], precision=highest
    )
    centre = reduced_rows[:, 4 * box_points : 5 * box_points]
    reduced = centre[:, skel_count:] - jnp.einsum(
        "rs,st->rt", centre[:, :skel_count], interp_box, precision=highest
    )
    diag_factor = jnp.linalg.cholesky(reduced)
    return jax.scipy.linalg.solve_triangular(diag_factor, reduced_rows, lower=True)


def spread(factor_new, move_first, move_second, p):
    box_points = factor_new.shape[1] // 9

    def take_block(m):
        k = block_of(m[0], m[1])
        return factor_new[:, k * box_points : (k + 1) * box_points]

    placed = {}
    section_one = {}
    for s in (1, -1):
        listing = [vector(u, v) for u in (0, s) for v in (-1, 0, 1)]
        arrived = move_first(jnp.stack([take_block(m) for m in listing]), s)
        source = vector(-s, 0)
        section_one[s] = (source, listing, arrived)
        for n, m in enumerate(listing):
            placed[source, (m[0] + source[0], m[1] + source[1])] = arrived[n]
    for t in (1, -1):
        payload = []
        labels = []
        for m in [vector(u, v) for u in (-1, 0, 1) for v in (0, t)]:
            payload.append(take_block(m))
            labels.append(((0, 0), m))
        for s in (1, -1):
            source, listing, arrived = section_one[s]
            for n, m in enumerate(listing):
                if m[1 - p] in (0, t):
                    payload.append(arrived[n])
                    labels.append((source, m))
        arrived = move_second(jnp.stack(payload), t)
        sender_at = vector(0, -t)
        for n, (anchor, m) in enumerate(labels):
            source = (anchor[0] + sender_at[0], anchor[1] + sender_at[1])
            placed[source, (m[0] + source[0], m[1] + source[1])] = arrived[n]
    for m in offsets_all():
        placed[(0, 0), m] = take_block(m)
    return jnp.stack([placed[pair] for pair in pairs_all()])


def on_device(offsets, point_order, nugget, interp):
    row_at = lax.axis_index("row")
    col_at = lax.axis_index("col")
    row_count = lax.axis_size("row")
    col_count = lax.axis_size("col")
    box_points = offsets.shape[3]
    skel_count = interp.shape[2]
    red_count = interp.shape[3]
    corner = jnp.stack([row_at, col_at]).astype(jnp.float32)[:, None]
    points = jnp.take(offsets[0, 0] + corner, point_order[0, 0], axis=1)
    weights = jnp.take(nugget[0, 0], point_order[0, 0])
    interp_box = interp[0, 0]
    neighbour_points = extended(points[None, None], (("row", 0), ("col", 1)), 1)
    present = []
    kernel_blocks = []
    for a, b in offsets_all():
        inside = (
            (row_at + a >= 0)
            & (row_at + a < row_count)
            & (col_at + b >= 0)
            & (col_at + b < col_count)
        )
        present.append(inside.astype(jnp.float32))
        kernel_block = kernel(points, neighbour_points[a + 1, b + 1]) * present[-1]
        if (a, b) == (0, 0):
            kernel_block = kernel_block + jnp.diag(weights)
        kernel_blocks.append(kernel_block)
    near_matrix = jnp.concatenate(kernel_blocks, axis=1)

    def move_first(x, amount):
        return shifted(x, "row", amount)

    def move_second(x, amount):
        return shifted(x, "col", amount)

    leading = 0
    colour = 2 * (row_at % 2) + col_at % 2
    stored = jnp.zeros((len(pairs_all()), red_count, box_points), jnp.float32)
    for k in range(4):
        factor_new = lax.cond(
            colour == k,
            lambda s: eliminate(s, near_matrix, interp_box),
            lambda s: jnp.zeros((red_count, 9 * box_points), jnp.float32),
            stored,
        )
        stored = stored + spread(factor_new, move_first, move_second, leading)
    row_width = skel_count // row_count
    col_width = skel_count // col_count
    box_total = row_count * col_count
    weights_skel = weights[:skel_count]
    row_ids = jnp.arange(skel_count, dtype=jnp.int32).reshape(row_count, row_width)
    col_ids = jnp.arange(skel_count, dtype=jnp.int32).reshape(col_count, col_width)
    diag_piece = jnp.where(
        row_ids[:, None, :, None] == col_ids[None, :, None, :],
        weights_skel.reshape(row_count, row_width)[:, None, :, None],
        0.0,
    )
    pieces = []
    for k, m in enumerate(offsets_all()):
        left_rows, right_rows = cross_pair(stored, m, skel_count)
        fill_part = jnp.einsum(
            "rak,rbl->abkl",
            left_rows.reshape(-1, row_count, row_width),
            right_rows.reshape(-1, col_count, col_width),
            precision=highest,
        )
        if m == (0, 0):
            delta_block = diag_piece - fill_part
        else:
            delta_block = -fill_part
        pieces.append(delta_block * present[k])
    outgoing = jnp.stack(pieces, axis=2).reshape(box_total * 9, row_width * col_width)
    arrived = lax.all_to_all(outgoing, ("row", "col"), split_axis=0, concat_axis=0, tiled=True)
    received = jnp.transpose(arrived.reshape(box_total, 9, row_width, col_width), (1, 2, 0, 3))
    box_ids = jnp.arange(box_total, dtype=jnp.int32)
    src_rows = (box_ids // col_count)[:, None]
    src_cols = (box_ids % col_count)[:, None]
    all_skeleton = lax.all_gather(points[:, :skel_count][None], ("row", "col"), axis=0, tiled=True)
    row_part = lax.dynamic_slice_in_dim(all_skeleton, row_at * row_width, row_width, 2)
    col_part = lax.dynamic_slice_in_dim(all_skeleton, col_at * col_width, col_width, 2)
    row_coords = jnp.transpose(row_part, (1, 2, 0)).reshape(2, row_width * box_total)
    col_coords = jnp.transpose(col_part, (1, 2, 0)).reshape(2, col_width * box_total)
    placed = jnp.zeros((row_width, box_total, col_width, box_total), jnp.float32)
    for n, (a, b) in enumerate(offsets_all()):
        target = (src_rows + a) * col_count + src_cols + b
        living = (
            (src_rows + a >= 0)
            & (src_rows + a < row_count)
            & (src_cols + b >= 0)
            & (src_cols + b < col_count)
        )
        hit = (target == box_ids[None, :]) & living
        placed = jnp.where(hit[None, :, None, :], received[n][:, :, :, None], placed)
    delta_tile = placed.reshape(row_width * box_total, col_width * box_total)
    root_matrix = kernel(row_coords, col_coords) + delta_tile
    rows_here = root_matrix.shape[0]
    cols_here = root_matrix.shape[1]
    global_rows = row_at * rows_here + jnp.arange(rows_here, dtype=jnp.int32)
    global_cols = col_at * cols_here + jnp.arange(cols_here, dtype=jnp.int32)
    columns_out = []
    for p in range(2):
        first_col = p * PW
        owner_col = first_col // cols_here
        local_col = first_col % cols_here
        owner_row = first_col // rows_here
        local_row = first_col % rows_here
        own_slab = root_matrix[:, local_col : local_col + PW]
        slab_rows = spread_2(own_slab, "col", owner_col)
        diag_block = spread_2(slab_rows[local_row : local_row + PW], "row", owner_row)
        diag_factor = jnp.linalg.cholesky(diag_block)
        solved = jax.scipy.linalg.solve_triangular(diag_factor, slab_rows.T, lower=True).T
        pasted = lax.dynamic_update_slice(solved, diag_factor, (first_col - row_at * rows_here, 0))
        inside = (global_rows >= first_col) & (global_rows < first_col + PW)
        panel_rows = jnp.where(
            (global_rows < first_col)[:, None], 0.0, jnp.where(inside[:, None], pasted, solved)
        )
        first_global = col_at * cols_here
        holder = first_global // rows_here
        offset_rows = first_global - holder * rows_here
        panel_cols = spread_2(
            lax.dynamic_slice_in_dim(panel_rows, offset_rows, cols_here, 0), "row", holder
        )
        root_matrix = root_matrix - jnp.einsum(
            "rk,ck->rc", panel_rows, panel_cols, precision=highest
        )
        columns_out.append((owner_col, local_col, panel_rows))
    for owner_col, local_col, panel_rows in columns_out:
        current = root_matrix[:, local_col : local_col + PW]
        root_matrix = lax.dynamic_update_slice(
            root_matrix, jnp.where(col_at == owner_col, panel_rows, current), (0, local_col)
        )
    top_rows = min(2 * PW, rows_here)
    top_block = root_matrix[:top_rows]
    zero_mask = (global_rows[:top_rows, None] < 2 * PW) & (global_cols[None, :] >= 2 * PW)
    return lax.dynamic_update_slice(root_matrix, jnp.where(zero_mask, 0.0, top_block), (0, 0))


def solution(mesh):
    in_specs = (
        P("row", "col", None, None),
        P("row", "col", None),
        P("row", "col", None),
        P("row", "col", None, None),
    )
    out_specs = P("row", "col")
    return jax.shard_map(
        on_device, mesh=mesh, in_specs=in_specs, out_specs=out_specs, check_vma=False
    )
```

profile of v0, /device:TPU:0, one launch (start us, length us, event | category | flops | bytes accessed | tf_op | source)
XLA Modules:
  0.0 1654.9 jit_solution(10580641799856505549)
XLA Ops:
  14.9 3.6 collective-permute-done.1
  18.5 3.5 collective-permute-start.2
  24.2 3.3 collective-permute-done.3
  29.1 55.5 %conditional.4 = (f32[128,256]{1,0:T(8,128)}, f32[128,256]{1,0:T(8,128)}, f32[128,256]{1,0:T(8,128)}, f32[128,256]{1,0:T(8,128)}, f32[128,256]{1,0:T(8,128)}, /*...) conditional(s32[]{:T(128)} %convert_element_type.56, () %tuple.65, ...), branch_computations={%region_0.1_spmd, %region_1.6_spmd} | conditional | flops 2442133504 | bytes 22315710 | solution.py:172
  39.8 13.2 cholesky.356
  56.6 11.3 custom-call.35
  86.0 2.9 copy.446
  109.8 4.6 collective-permute-done.5
  119.9 29.2 %collective-permute-done.6 = f32[14,128,256]{2,1,0:T(8,128)} collective-permute-done((f32[14,128,256]{2,1,0:T(8,128)}, f32[14,128,256]{2,1,0:T(8,128)}, u32[]{:S(2)}, u32[]{:S(2)}) %collective-permute-start.6) | collective-permute-done | bytes 1835040 | tf_op jit(solution)/shard_map/ppermute | solution.py:28
  151.4 3.5 collective-permute-done.7
  168.6 8.2 conditional.5
  185.9 10.8 collective-permute-start.8
  201.8 7.9 collective-permute-done.9
  209.8 57.6 %collective-permute-start.10 = (f32[14,128,256]{2,1,0:T(8,128)S(1)}, f32[14,128,256]{2,1,0:T(8,128)S(1)}, u32[]{:S(2)}, u32[]{:S(2)}) collective-permute-start(f32[14,128,256]{2,1,0:T(8,128)S(1)} %get-tuple-element.880), channel_id=1, source_target_pairs={{0,1},{1,2},{2,3},{3,4},{4,5},{5,6},{6,7},{7,8},{8,9},{9,10},{10,1... | collective-permute-start | bytes 5505032 | tf_op jit(solution)/shard_map/ppermute | solution.py:28
  274.5 24.2 %collective-permute-done.10 = f32[14,128,256]{2,1,0:T(8,128)S(1)} collective-permute-done((f32[14,128,256]{2,1,0:T(8,128)S(1)}, f32[14,128,256]{2,1,0:T(8,128)S(1)}, u32[]{:S(2)}, u32[]{:S(2)}) %collective-permute-start.10) | collective-permute-done | bytes 1835040 | tf_op jit(solution)/shard_map/ppermute | solution.py:28
  298.8 5.6 collective-permute-done.11
  311.3 3.7 add.655
  315.1 9.1 conditional.6
  325.8 3.0 copy.582
  343.4 70.5 %collective-permute-start.12 = (f32[6,128,256]{2,1,0:T(8,128)S(1)}, f32[6,128,256]{2,1,0:T(8,128)S(1)}, u32[]{:S(2)}, u32[]{:S(2)}) collective-permute-start(f32[6,128,256]{2,1,0:T(8,128)S(1)} %get-tuple-element.968), channel_id=1, source_target_pairs={{0,16},{16,32},{32,48},{48,64},{64,80},{80,96},{96,112},{1,17},{17... | collective-permute-start | bytes 2359304 | tf_op jit(solution)/shard_map/ppermute | solution.py:28
  427.8 106.3 %all-gather.1 = f32[128,2,128]{2,1,0:T(2,128)S(1)} all-gather(f32[1,2,128]{2,1,0:T(2,128)S(1)} %copy.132), channel_id=2, replica_groups=mesh['row'=8,'col'=16] {'row','col'}, dimensions={0}, use_global_device_ids=true | all-gather | bytes 132096 | tf_op jit(solution)/shard_map/all_gather | solution.py:210
  560.8 6.9 add.656
  567.7 10.7 conditional.7
  597.4 51.3 %collective-permute-start.18 = (f32[14,128,256]{2,1,0:T(8,128)}, f32[14,128,256]{2,1,0:T(8,128)}, u32[]{:S(2)}, u32[]{:S(2)}) collective-permute-start(f32[14,128,256]{2,1,0:T(8,128)} %get-tuple-element.864), channel_id=1, source_target_pairs={{0,1},{1,2},{2,3},{3,4},{4,5},{5,6},{6,7},{7,8},{8,9},{9,10},{10,1... | collective-permute-start | bytes 5505032 | tf_op jit(solution)/shard_map/ppermute | solution.py:28
  661.2 18.5 %collective-permute-done.18 = f32[14,128,256]{2,1,0:T(8,128)} collective-permute-done((f32[14,128,256]{2,1,0:T(8,128)}, f32[14,128,256]{2,1,0:T(8,128)}, u32[]{:S(2)}, u32[]{:S(2)}) %collective-permute-start.18) | collective-permute-done | bytes 1835040 | tf_op jit(solution)/shard_map/ppermute | solution.py:28
  680.9 8.0 collective-permute-done.19
  693.5 4.1 add.657
  730.9 3.6 fusion.239
  755.3 20.8 %all-to-all-start = ((f32[128,9,128]{2,1,0:T(8,128)}), f32[128,9,128]{2,1,0:T(8,128)S(1)}, u32[]{:S(2)}, u32[]{:S(2)}) async-start(f32[128,9,128]{2,1,0:T(8,128)} %copy.165), calls=%async_computation | async-start | bytes 2097152 | tf_op jit(solution)/shard_map/all_to_all | solution.py:205
  776.4 18.7 %all-to-all-done = f32[128,9,128]{2,1,0:T(8,128)S(1)} async-done(((f32[128,9,128]{2,1,0:T(8,128)}), f32[128,9,128]{2,1,0:T(8,128)S(1)}, u32[]{:S(2)}, u32[]{:S(2)}) %all-to-all-start) | async-done | bytes 589856 | tf_op jit(solution)/shard_map/all_to_all | solution.py:205
  795.8 5.4 select_select_fusion.4
  801.2 6.1 bitcast_add_fusion.4
  807.3 3.4 copy-done.2
  813.4 98.8 %all-reduce.10.cloned.1.call-done = f32[2048,512]{0,1:T(8,128)} async-done(((f32[2048,512]{0,1:T(8,128)}), f32[2048,512]{0,1:T(8,128)}) %all-reduce.10.cloned.1.call-update) | async-done | bytes 4194320 | tf_op jit(solution)/shard_map/psum | solution.py:33
  915.0 62.4 %all-reduce.12.cloned.1.call-done = f32[512,512]{0,1:T(8,128)} async-done(((f32[512,512]{0,1:T(8,128)}), f32[512,512]{0,1:T(8,128)}) %all-reduce.12.cloned.1.call-update) | async-done | bytes 1048592 | tf_op jit(solution)/shard_map/psum | solution.py:33
  979.3 11.7 cholesky.402
  991.0 9.8 custom-call.39
  1001.5 11.7 cholesky.421
  1013.6 10.3 custom-call.40
  1024.9 11.7 cholesky.442
  1036.8 9.8 custom-call.41
  1047.4 11.9 cholesky.459
  1064.7 8.2 while.4
  1072.8 39.3 %custom-call.42 = f32[4,128,128]{1,2,0:T(8,128)S(1)} custom-call(f32[4,128,128]{2,1,0:T(8,128)S(1)} %get-tuple-element.489), custom_call_target="InvertDiagBlocksLowerTriangular" | custom-call | tf_op jit(solution)/shard_map/jit(_solve_triangular)/triangular_solve | solution.py:243
  1130.4 65.2 %all-reduce.14.cloned.1.call-done = f32[1024,512]{0,1:T(8,128)} async-done(((f32[1024,512]{0,1:T(8,128)}), f32[1024,512]{0,1:T(8,128)}) %all-reduce.14.cloned.1.call-update) | async-done | bytes 2097168 | tf_op jit(solution)/shard_map/psum | solution.py:33
  1195.6 17.6 %convolution_subtract_fusion.5 = f32[2048,1024]{0,1:T(8,128)S(1)} fusion(f32[2048,1024]{0,1:T(8,128)} %copy-done.2, f32[2048,512]{0,1:T(8,128)} %copy-done.9, f32[1024,512]{0,1:T(8,128)} %all-reduce.14.cloned.1.call-done), kind=kOutput, calls=%fused_computation.563 | convolution fusion | flops 12886999040 | bytes 23068672 | tf_op jit(solution)/shard_map/rk,ck->rc/dot_general | solution.py:255
  1213.2 3.4 copy-done.3
  1219.0 102.7 %all-reduce.16.cloned.1.call-done = f32[2048,512]{0,1:T(8,128)} async-done(((f32[2048,512]{0,1:T(8,128)}), f32[2048,512]{0,1:T(8,128)}) %all-reduce.16.cloned.1.call-update) | async-done | bytes 4194320 | tf_op jit(solution)/shard_map/psum | solution.py:33
  1324.1 62.7 %all-reduce.18.cloned.1.call-done = f32[512,512]{0,1:T(8,128)} async-done(((f32[512,512]{0,1:T(8,128)}), f32[512,512]{0,1:T(8,128)}) %all-reduce.18.cloned.1.call-update) | async-done | bytes 1048592 | tf_op jit(solution)/shard_map/psum | solution.py:33
  1388.8 11.7 cholesky.474
  1400.5 9.8 custom-call.43
  1411.0 11.7 cholesky.493
  1423.1 10.0 custom-call.44
  1434.1 11.7 cholesky.514
  1446.0 9.8 custom-call.45
  1456.6 11.9 cholesky.531
  1473.9 8.3 while.5
  1482.2 39.3 %custom-call.46 = f32[4,128,128]{1,2,0:T(8,128)S(1)} custom-call(f32[4,128,128]{2,1,0:T(8,128)S(1)} %get-tuple-element.490), custom_call_target="InvertDiagBlocksLowerTriangular" | custom-call | tf_op jit(solution)/shard_map/jit(_solve_triangular)/triangular_solve | solution.py:243
  1539.7 65.4 %all-reduce.20.cloned.1.call-done = f32[1024,512]{0,1:T(8,128)} async-done(((f32[1024,512]{0,1:T(8,128)}), f32[1024,512]{0,1:T(8,128)}) %all-reduce.20.cloned.1.call-update) | async-done | bytes 2097168 | tf_op jit(solution)/shard_map/psum | solution.py:33
  1605.1 18.3 %convolution_subtract_fusion.4 = f32[2048,1024]{0,1:T(8,128)} fusion(f32[2048,1024]{0,1:T(8,128)} %copy-done.3, f32[2048,512]{0,1:T(8,128)} %copy-done.8, f32[1024,512]{0,1:T(8,128)} %all-reduce.20.cloned.1.call-done), kind=kOutput, calls=%fused_computation.562 | convolution fusion | flops 12886999040 | bytes 23068672 | tf_op jit(solution)/shard_map/rk,ck->rc/dot_general | solution.py:255
  1623.4 5.2 fusion.213
  1628.7 5.1 fusion.212
  1633.8 4.7 fusion.211
  1638.5 9.3 copy.196
  (753 shorter events, 350.8 us)
Async XLA Ops:
  11.6 3.1 collective-permute-start
  13.0 5.5 collective-permute-start.1
  14.4 9.3 copy-start.39
  18.5 5.2 collective-permute-start.2
  22.0 5.5 collective-permute-start.3
  92.0 13.8 copy-start.29
  103.5 4.5 collective-permute-start.4
  106.7 7.7 collective-permute-start.5
  108.0 6.4 copy-start.10
  116.0 33.0 %collective-permute-start.6 = (f32[14,128,256]{2,1,0:T(8,128)}, f32[14,128,256]{2,1,0:T(8,128)}, u32[]{:S(2)}, u32[]{:S(2)}) collective-permute-start(f32[14,128,256]{2,1,0:T(8,128)} %get-tuple-element.888), channel_id=1, source_target_pairs={{0,1},{1,2},{2,3},{3,4},{4,5},{5,6},{6,7},{7,8},{8,9},{9,10},{10,1... | collective-permute-start | bytes 5505032 | tf_op jit(solution)/shard_map/ppermute | solution.py:28
  118.6 36.2 %collective-permute-start.7 = (f32[14,128,256]{2,1,0:T(8,128)}, f32[14,128,256]{2,1,0:T(8,128)}, u32[]{:S(2)}, u32[]{:S(2)}) collective-permute-start(f32[14,128,256]{2,1,0:T(8,128)} %get-tuple-element.887), channel_id=1, source_target_pairs={{1,0},{2,1},{3,2},{4,3},{5,4},{6,5},{7,6},{8,7},{9,8},{10,9},{11,1... | collective-permute-start | bytes 5505032 | tf_op jit(solution)/shard_map/ppermute | solution.py:28
  157.1 8.8 copy-start.11
  157.1 8.8 copy-start.18
  177.7 21.2 %copy-start.13 = (f32[49,128,256]{2,1,0:T(8,128)S(1)}, f32[49,128,256]{2,1,0:T(8,128)}, u32[]{:S(2)}) copy-start(f32[49,128,256]{2,1,0:T(8,128)} %copy-done.12) | copy-start | bytes 19267588
  185.9 15.8 collective-permute-start.8
  197.6 12.1 collective-permute-start.9
  209.8 88.9 %collective-permute-start.10 = (f32[14,128,256]{2,1,0:T(8,128)S(1)}, f32[14,128,256]{2,1,0:T(8,128)S(1)}, u32[]{:S(2)}, u32[]{:S(2)}) collective-permute-start(f32[14,128,256]{2,1,0:T(8,128)S(1)} %get-tuple-element.880), channel_id=1, source_target_pairs={{0,1},{1,2},{2,3},{3,4},{4,5},{5,6},{6,7},{7,8},{8,9},{9,10},{10,1... | collective-permute-start | bytes 5505032 | tf_op jit(solution)/shard_map/ppermute | solution.py:28
  268.3 36.1 %collective-permute-start.11 = (f32[14,128,256]{2,1,0:T(8,128)S(1)}, f32[14,128,256]{2,1,0:T(8,128)S(1)}, u32[]{:S(2)}, u32[]{:S(2)}) collective-permute-start(f32[14,128,256]{2,1,0:T(8,128)S(1)} %get-tuple-element.879), channel_id=1, source_target_pairs={{1,0},{2,1},{3,2},{4,3},{5,4},{6,5},{7,6},{8,7},{9,8},{10,9},{11,1... | collective-permute-start | bytes 5505032 | tf_op jit(solution)/shard_map/ppermute | solution.py:28
  343.4 74.6 %collective-permute-start.12 = (f32[6,128,256]{2,1,0:T(8,128)S(1)}, f32[6,128,256]{2,1,0:T(8,128)S(1)}, u32[]{:S(2)}, u32[]{:S(2)}) collective-permute-start(f32[6,128,256]{2,1,0:T(8,128)S(1)} %get-tuple-element.968), channel_id=1, source_target_pairs={{0,16},{16,32},{32,48},{48,64},{64,80},{80,96},{96,112},{1,17},{17... | collective-permute-start | bytes 2359304 | tf_op jit(solution)/shard_map/ppermute | solution.py:28
  414.8 10.9 copy-start.81
  414.8 12.9 copy-start.40
  416.7 4.2 collective-permute-start.13
  422.6 115.9 %collective-permute-start.14 = (f32[14,128,256]{2,1,0:T(8,128)}, f32[14,128,256]{2,1,0:T(8,128)}, u32[]{:S(2)}, u32[]{:S(2)}) collective-permute-start(f32[14,128,256]{2,1,0:T(8,128)} %get-tuple-element.872), channel_id=1, source_target_pairs={{0,1},{1,2},{2,3},{3,4},{4,5},{5,6},{6,7},{7,8},{8,9},{9,10},{10,1... | collective-permute-start | bytes 5505032 | tf_op jit(solution)/shard_map/ppermute | solution.py:28
  426.5 114.3 %collective-permute-start.15 = (f32[14,128,256]{2,1,0:T(8,128)}, f32[14,128,256]{2,1,0:T(8,128)}, u32[]{:S(2)}, u32[]{:S(2)}) collective-permute-start(f32[14,128,256]{2,1,0:T(8,128)} %get-tuple-element.871), channel_id=1, source_target_pairs={{1,0},{2,1},{3,2},{4,3},{5,4},{6,5},{7,6},{8,7},{9,8},{10,9},{11,1... | collective-permute-start | bytes 5505032 | tf_op jit(solution)/shard_map/ppermute | solution.py:28
  560.8 6.9 copy-start.19
  586.6 7.0 copy-start.82
  586.6 7.0 copy-start.83
  589.7 4.5 collective-permute-start.16
  591.7 4.2 collective-permute-start.17
  597.4 82.3 %collective-permute-start.18 = (f32[14,128,256]{2,1,0:T(8,128)}, f32[14,128,256]{2,1,0:T(8,128)}, u32[]{:S(2)}, u32[]{:S(2)}) collective-permute-start(f32[14,128,256]{2,1,0:T(8,128)} %get-tuple-element.864), channel_id=1, source_target_pairs={{0,1},{1,2},{2,3},{3,4},{4,5},{5,6},{6,7},{7,8},{8,9},{9,10},{10,1... | collective-permute-start | bytes 5505032 | tf_op jit(solution)/shard_map/ppermute | solution.py:28
  652.4 36.5 %collective-permute-start.19 = (f32[14,128,256]{2,1,0:T(8,128)S(1)}, f32[14,128,256]{2,1,0:T(8,128)S(1)}, u32[]{:S(2)}, u32[]{:S(2)}) collective-permute-start(f32[14,128,256]{2,1,0:T(8,128)S(1)} %get-tuple-element.863), channel_id=1, source_target_pairs={{1,0},{2,1},{3,2},{4,3},{5,4},{6,5},{7,6},{8,7},{9,8},{10,9},{11,1... | collective-permute-start | bytes 5505032 | tf_op jit(solution)/shard_map/ppermute | solution.py:28
  680.8 9.4 copy-start.38
  680.8 9.4 copy-start.32
  680.8 9.4 copy-start.35
  680.8 9.4 copy-start.49
  680.8 9.5 copy-start.43
  680.9 10.3 copy-start.27
  680.9 10.4 copy-start.46
  716.8 6.0 copy-start.67
  717.6 5.8 copy-start.66
  718.5 6.2 copy-start.64
  724.7 5.9 copy-start.52
  730.8 10.2 copy-start.61
  730.9 10.2 copy-start.60
  730.9 10.2 copy-start.63
  730.9 10.2 copy-start.62
  753.6 22.6 %copy-start.54 = (f32[128,2,16]{2,1,0:T(2,128)S(1)}, f32[128,2,16]{2,1,0:T(2,128)}, u32[]{:S(2)}) copy-start(f32[128,2,16]{2,1,0:T(2,128)} %constant_dynamic-slice_fusion.5) | copy-start | bytes 49156
  755.3 39.8 %all-to-all-start = ((f32[128,9,128]{2,1,0:T(8,128)}), f32[128,9,128]{2,1,0:T(8,128)S(1)}, u32[]{:S(2)}, u32[]{:S(2)}) async-start(f32[128,9,128]{2,1,0:T(8,128)} %copy.165), calls=%async_computation | async-start | bytes 2097152 | tf_op jit(solution)/shard_map/all_to_all | solution.py:205
  776.1 19.6 %copy-start.73 = (pred[128,128]{0,1:T(8,128)(4,1)S(1)}, pred[128,128]{0,1:T(8,128)(4,1)}, u32[]{:S(2)}) copy-start(pred[128,128]{0,1:T(8,128)(4,1)} %fusion.311) | copy-start | bytes 49156
  776.1 19.6 %copy-start.74 = (pred[128,128]{0,1:T(8,128)(4,1)S(1)}, pred[128,128]{0,1:T(8,128)(4,1)}, u32[]{:S(2)}) copy-start(pred[128,128]{0,1:T(8,128)(4,1)} %fusion.312) | copy-start | bytes 49156
  776.1 19.6 %copy-start.75 = (pred[128,128]{0,1:T(8,128)(4,1)S(1)}, pred[128,128]{0,1:T(8,128)(4,1)}, u32[]{:S(2)}) copy-start(pred[128,128]{0,1:T(8,128)(4,1)} %fusion.313) | copy-start | bytes 49156
  776.1 19.6 %copy-start.76 = (pred[128,128]{0,1:T(8,128)(4,1)S(1)}, pred[128,128]{0,1:T(8,128)(4,1)}, u32[]{:S(2)}) copy-start(pred[128,128]{0,1:T(8,128)(4,1)} %fusion.314) | copy-start | bytes 49156
  776.1 19.6 %copy-start.77 = (pred[128,128]{0,1:T(8,128)(4,1)S(1)}, pred[128,128]{0,1:T(8,128)(4,1)}, u32[]{:S(2)}) copy-start(pred[128,128]{0,1:T(8,128)(4,1)} %fusion.315) | copy-start | bytes 49156
  776.2 19.6 %copy-start.78 = (pred[128,128]{0,1:T(8,128)(4,1)S(1)}, pred[128,128]{0,1:T(8,128)(4,1)}, u32[]{:S(2)}) copy-start(pred[128,128]{0,1:T(8,128)(4,1)} %fusion.316) | copy-start | bytes 49156
  776.2 19.6 %copy-start.79 = (pred[128,128]{0,1:T(8,128)(4,1)S(1)}, pred[128,128]{0,1:T(8,128)(4,1)}, u32[]{:S(2)}) copy-start(pred[128,128]{0,1:T(8,128)(4,1)} %fusion.317) | copy-start | bytes 49156
  776.2 19.6 %copy-start.80 = (pred[128,128]{0,1:T(8,128)(4,1)S(1)}, pred[128,128]{0,1:T(8,128)(4,1)}, u32[]{:S(2)}) copy-start(pred[128,128]{0,1:T(8,128)(4,1)} %fusion.318) | copy-start | bytes 49156
  776.2 136.0 %all-reduce.10.cloned.1.call-start = ((), (), s32[]{:S(2)}) async-start(), calls=%async_computation.1 | async-start | bytes 8388608 | tf_op jit(solution)/shard_map/psum | solution.py:33
  813.3 164.0 %all-reduce.12.cloned.1.call-start = ((), (), s32[]{:S(2)}) async-start(), calls=%async_computation.2 | async-start | bytes 2097152 | tf_op jit(solution)/shard_map/psum | solution.py:33
  914.6 281.0 %all-reduce.14.cloned.1.call-start = ((), (), s32[]{:S(2)}) async-start(), calls=%async_computation.3 | async-start | bytes 4194304 | tf_op jit(solution)/shard_map/psum | solution.py:33
  1130.4 191.3 %all-reduce.16.cloned.1.call-start = ((), (), s32[]{:S(2)}) async-start(), calls=%async_computation.4 | async-start | bytes 8388608 | tf_op jit(solution)/shard_map/psum | solution.py:33
  1219.0 167.9 %all-reduce.18.cloned.1.call-start = ((), (), s32[]{:S(2)}) async-start(), calls=%async_computation.5 | async-start | bytes 2097152 | tf_op jit(solution)/shard_map/psum | solution.py:33
  1324.1 281.0 %all-reduce.20.cloned.1.call-start = ((), (), s32[]{:S(2)}) async-start(), calls=%async_computation.6 | async-start | bytes 4194304 | tf_op jit(solution)/shard_map/psum | solution.py:33
  1605.1 18.3 %copy-start.7 = (f32[2048,512]{0,1:T(8,128)S(1)}, f32[2048,512]{0,1:T(8,128)}, u32[]{:S(2)}) copy-start(f32[2048,512]{0,1:T(8,128)} %copy-done.6) | copy-start | bytes 12582916
  1638.5 9.3 copy-start.1
  (44 other events, 103.3 us)
Sparse Core Ops, SparseCore 0:
  813.4 98.7 all-reduce.9
  914.7 62.6 all-reduce.11
  1130.5 65.0 all-reduce.13
  1219.1 102.5 all-reduce.15
  1324.2 62.6 all-reduce.17
  1539.8 65.2 all-reduce.19
where the time goes:
time: 1660 us; the launch traced here: 1650 us
  waiting for transfers between devices  586 us (35%)
  other arithmetic  345 us (21%)
  local copies, waits for them, and re-layouts  257 us (15%)
  starting transfers between devices  237 us (14%)
  blocking collectives  106 us (6%)
  matrix products  85.1 us (5%)
  between operations  22.1 us (1%)
  loops' own time  17.7 us (1%)
    psum x6, waiting for transfers between devices, spread_2(): return lax.psum(kept, axis)  457 us
    ppermute x16, starting transfers between devices, shifted(): return lax.ppermute(block, axis, route)  208 us
    another operation x30, other arithmetic, on_device(): diag_factor = jnp.linalg.cholesky(diag_block)  159 us
    unnamed x365, local copies, waits for them, and re-layouts  152 us
    all_gather x1, blocking collectives, on_device(): lax.all_gather(points[:, :skel_count][None], ('row', 'col'), axis=0, tile...  106 us
    ppermute x16, waiting for transfers between devices, shifted(): return lax.ppermute(block, axis, route)  103 us
    another operation x7, other arithmetic, on_device(): jax.scipy.linalg.solve_triangular(diag_factor, slab_rows.T, lower=True)  81 us
    dot_general x2, matrix products, on_device(): jnp.einsum('rk,ck->rc', panel_rows, panel_cols, precision=highest)  35.9 us
  transfers between devices with their start and end apart: 27, of which 19 were waited for; matrix products, arithmetic and copies ran while one was open for 3% of the time, Pallas kernels for 0%

commit v1 on v0

--- a/solution.py
+++ b/solution.py
@@ -30,7 +30,7 @@
 
 def spread_2(value, axis, source):
     kept = jnp.where(lax.axis_index(axis) == source, value, 0).astype(value.dtype)
-    return lax.psum(kept, axis)
+    return jnp.sum(lax.all_gather(kept, axis), axis=0)
 
 
 def offsets_all():

time: 1660 us -> 2310 us (1.39)
  waiting for transfers between devices: 586 us -> 1120 us
  other arithmetic: 345 us -> 425 us
    all_gather x0 -> x6, waiting for transfers between devices: none -> 991 us  [spread_2(): return jnp.sum(lax.all_gather(kept, axis), axis=0)]
    psum x6 -> x0, waiting for transfers between devices: 457 us -> none  [spread_2(): return lax.psum(kept, axis)]
    reduce_sum x0 -> x6, other arithmetic: none -> 71.7 us  [spread_2(): return jnp.sum(lax.all_gather(kept, axis), axis=0)]
    unnamed x365 -> x396, local copies, waits for them, and re-layouts: 152 us -> 155 us
where the time goes in v1:
time: 2310 us; the launch traced here: 2300 us
  waiting for transfers between devices  1120 us (48%)
  other arithmetic  425 us (18%)
  local copies, waits for them, and re-layouts  275 us (12%)
  starting transfers between devices  237 us (10%)
  blocking collectives  106 us (5%)
  matrix products  98.5 us (4%)
    all_gather x6, waiting for transfers between devices, spread_2(): return jnp.sum(lax.all_gather(kept, axis), axis=0)  991 us
    ppermute x16, starting transfers between devices, shifted(): return lax.ppermute(block, axis, route)  208 us
    another operation x30, other arithmetic, on_device(): diag_factor = jnp.linalg.cholesky(diag_block)  159 us
    unnamed x396, local copies, waits for them, and re-layouts  155 us
    all_gather x1, blocking collectives, on_device(): lax.all_gather(points[:, :skel_count][None], ('row', 'col'), axis=0, tile...  106 us
    ppermute x16, waiting for transfers between devices, shifted(): return lax.ppermute(block, axis, route)  102 us
    another operation x7, other arithmetic, on_device(): jax.scipy.linalg.solve_triangular(diag_factor, slab_rows.T, lower=True)  80 us
    reduce_sum x6, other arithmetic, spread_2(): return jnp.sum(lax.all_gather(kept, axis), axis=0)  71.7 us
  transfers between devices with their start and end apart: 27, of which 19 were waited for; matrix products, arithmetic and copies ran while one was open for 3% of the time, Pallas kernels for 0%

profile of v1, /device:TPU:0, one launch (start us, length us, event | category | flops | bytes accessed | tf_op | source)
XLA Modules:
  0.0 2299.4 jit_solution(16106179558600103911)
XLA Ops:
  14.9 3.6 collective-permute-done.1
  18.5 3.5 collective-permute-start.2
  29.1 55.4 %conditional.4 = (f32[128,256]{1,0:T(8,128)}, f32[128,256]{1,0:T(8,128)}, f32[128,256]{1,0:T(8,128)}, f32[128,256]{1,0:T(8,128)}, f32[128,256]{1,0:T(8,128)}, /*...) conditional(s32[]{:T(128)} %convert_element_type.56, () %tuple.65, ...), branch_computations={%region_0.1_spmd, %region_1.6_spmd} | conditional | flops 2442133504 | bytes 22315710 | solution.py:172
  39.5 13.2 cholesky.356
  56.4 11.3 custom-call.35
  109.7 4.6 collective-permute-done.5
  119.8 29.2 %collective-permute-done.6 = f32[14,128,256]{2,1,0:T(8,128)} collective-permute-done((f32[14,128,256]{2,1,0:T(8,128)}, f32[14,128,256]{2,1,0:T(8,128)}, u32[]{:S(2)}, u32[]{:S(2)}) %collective-permute-start.6) | collective-permute-done | bytes 1835040 | tf_op jit(solution)/shard_map/ppermute | solution.py:28
  168.5 8.0 conditional.5
  185.6 10.8 collective-permute-start.8
  201.5 7.9 collective-permute-done.9
  209.5 57.7 %collective-permute-start.10 = (f32[14,128,256]{2,1,0:T(8,128)S(1)}, f32[14,128,256]{2,1,0:T(8,128)S(1)}, u32[]{:S(2)}, u32[]{:S(2)}) collective-permute-start(f32[14,128,256]{2,1,0:T(8,128)S(1)} %get-tuple-element.856), channel_id=1, source_target_pairs={{0,1},{1,2},{2,3},{3,4},{4,5},{5,6},{6,7},{7,8},{8,9},{9,10},{10,1... | collective-permute-start | bytes 5505032 | tf_op jit(solution)/shard_map/ppermute | solution.py:28
  274.3 24.2 %collective-permute-done.10 = f32[14,128,256]{2,1,0:T(8,128)S(1)} collective-permute-done((f32[14,128,256]{2,1,0:T(8,128)S(1)}, f32[14,128,256]{2,1,0:T(8,128)S(1)}, u32[]{:S(2)}, u32[]{:S(2)}) %collective-permute-start.10) | collective-permute-done | bytes 1835040 | tf_op jit(solution)/shard_map/ppermute | solution.py:28
  298.6 5.6 collective-permute-done.11
  311.1 3.7 add.643
  314.8 9.4 conditional.6
  343.4 70.5 %collective-permute-start.12 = (f32[6,128,256]{2,1,0:T(8,128)S(1)}, f32[6,128,256]{2,1,0:T(8,128)S(1)}, u32[]{:S(2)}, u32[]{:S(2)}) collective-permute-start(f32[6,128,256]{2,1,0:T(8,128)S(1)} %get-tuple-element.944), channel_id=1, source_target_pairs={{0,16},{16,32},{32,48},{48,64},{64,80},{80,96},{96,112},{1,17},{17... | collective-permute-start | bytes 2359304 | tf_op jit(solution)/shard_map/ppermute | solution.py:28
  427.9 106.3 %all-gather.7 = f32[128,2,128]{2,1,0:T(2,128)S(1)} all-gather(f32[1,2,128]{2,1,0:T(2,128)S(1)} %copy.238), channel_id=2, replica_groups=mesh['row'=8,'col'=16] {'row','col'}, dimensions={0}, use_global_device_ids=true | all-gather | bytes 132096 | tf_op jit(solution)/shard_map/all_gather | solution.py:210
  561.0 6.9 add.644
  567.9 10.6 conditional.7
  597.6 51.1 %collective-permute-start.18 = (f32[14,128,256]{2,1,0:T(8,128)}, f32[14,128,256]{2,1,0:T(8,128)}, u32[]{:S(2)}, u32[]{:S(2)}) collective-permute-start(f32[14,128,256]{2,1,0:T(8,128)} %get-tuple-element.840), channel_id=1, source_target_pairs={{0,1},{1,2},{2,3},{3,4},{4,5},{5,6},{6,7},{7,8},{8,9},{9,10},{10,1... | collective-permute-start | bytes 5505032 | tf_op jit(solution)/shard_map/ppermute | solution.py:28
  661.9 17.8 collective-permute-done.18
  680.9 8.0 collective-permute-done.19
  693.5 4.1 add.645
  746.7 20.7 all-to-all-start
  768.9 17.6 all-to-all-done
  797.4 21.9 select_select_fusion.4
  819.4 5.0 bitcast_add_fusion.4
  830.6 363.9 %all-gather.15.cloned.1.call-done = f32[32768,512]{1,0:T(8,128)} async-done(((f32[2048,512]{1,0:T(8,128)}), f32[32768,512]{1,0:T(8,128)}) %all-gather.15.cloned.1.call-update) | async-done | bytes 67108880 | tf_op jit(solution)/shard_map/all_gather | solution.py:33
  1194.5 23.1 %reduce_sum.54 = f32[2048,512]{1,0:T(8,128)} reduce(f32[16,2048,512]{2,1,0:T(8,128)} %bitcast.335, f32[]{:T(128)} %constant.345.clone.1), dimensions={0}, to_apply=%region_10.13 | reduce | flops 15728640 | bytes 71303168 | tf_op jit(solution)/shard_map/reduce_sum | solution.py:33
  1220.1 5.6 copy.283
  1225.7 44.0 %all-gather.17.cloned.1.call-done = f32[4096,512]{1,0:T(8,128)} async-done(((f32[512,512]{1,0:T(8,128)}), f32[4096,512]{1,0:T(8,128)}) %all-gather.17.cloned.1.call-update) | async-done | bytes 8388624 | tf_op jit(solution)/shard_map/all_gather | solution.py:33
  1269.7 4.6 reduce_sum.55
  1275.8 11.7 cholesky.402
  1287.7 9.8 custom-call.39
  1300.0 12.1 cholesky.421
  1313.5 9.8 custom-call.40
  1324.9 11.7 cholesky.442
  1337.3 9.8 custom-call.41
  1348.6 11.9 cholesky.459
  1363.8 8.3 while.4
  1372.1 39.3 %custom-call.42 = f32[4,128,128]{1,2,0:T(8,128)S(1)} custom-call(f32[4,128,128]{2,1,0:T(8,128)S(1)} %get-tuple-element.489), custom_call_target="InvertDiagBlocksLowerTriangular" | custom-call | tf_op jit(solution)/shard_map/jit(_solve_triangular)/triangular_solve | solution.py:243
  1421.5 4.0 fusion.229
  1440.8 84.9 %all-gather.19.cloned.1.call-done = f32[8192,512]{1,0:T(8,128)} async-done(((f32[1024,512]{1,0:T(8,128)}), f32[8192,512]{1,0:T(8,128)}) %all-gather.19.cloned.1.call-update) | async-done | bytes 16777232 | tf_op jit(solution)/shard_map/all_gather | solution.py:33
  1525.7 8.2 reduce_sum.56
  1533.9 16.6 convolution_subtract_fusion.5
  1556.5 368.9 %all-gather.21.cloned.1.call-done = f32[32768,512]{1,0:T(8,128)} async-done(((f32[2048,512]{1,0:T(8,128)}), f32[32768,512]{1,0:T(8,128)}) %all-gather.21.cloned.1.call-update) | async-done | bytes 67108880 | tf_op jit(solution)/shard_map/all_gather | solution.py:33
  1925.4 23.1 %reduce_sum.57 = f32[2048,512]{1,0:T(8,128)} reduce(f32[16,2048,512]{2,1,0:T(8,128)} %bitcast.352, f32[]{:T(128)} %constant.345.clone.1), dimensions={0}, to_apply=%region_21.26 | reduce | flops 15728640 | bytes 71303168 | tf_op jit(solution)/shard_map/reduce_sum | solution.py:33
  1951.0 5.6 copy.289
  1956.5 44.1 %all-gather.23.cloned.1.call-done = f32[4096,512]{1,0:T(8,128)} async-done(((f32[512,512]{1,0:T(8,128)}), f32[4096,512]{1,0:T(8,128)}) %all-gather.23.cloned.1.call-update) | async-done | bytes 8388624 | tf_op jit(solution)/shard_map/all_gather | solution.py:33
  2000.6 4.6 reduce_sum.58
  2006.8 11.7 cholesky.474
  2018.6 9.8 custom-call.43
  2031.0 12.1 cholesky.493
  2044.4 9.8 custom-call.44
  2055.8 11.7 cholesky.514
  2068.2 9.8 custom-call.45
  2079.5 11.9 cholesky.531
  2094.8 7.7 while.5
  2102.6 39.3 %custom-call.46 = f32[4,128,128]{1,2,0:T(8,128)S(1)} custom-call(f32[4,128,128]{2,1,0:T(8,128)S(1)} %get-tuple-element.490), custom_call_target="InvertDiagBlocksLowerTriangular" | custom-call | tf_op jit(solution)/shard_map/jit(_solve_triangular)/triangular_solve | solution.py:243
  2151.9 4.0 fusion.226
  2170.9 85.3 %all-gather.25.cloned.1.call-done = f32[8192,512]{1,0:T(8,128)} async-done(((f32[1024,512]{1,0:T(8,128)}), f32[8192,512]{1,0:T(8,128)}) %all-gather.25.cloned.1.call-update) | async-done | bytes 16777232 | tf_op jit(solution)/shard_map/all_gather | solution.py:33
  2256.1 8.2 reduce_sum.59
  2264.3 16.8 convolution_subtract_fusion.4
  2287.7 4.7 fusion.211
  (764 shorter events, 402.3 us)
Async XLA Ops:
  11.6 3.1 collective-permute-start
  13.0 5.5 collective-permute-start.1
  14.4 9.3 copy-start.50
  18.5 5.2 collective-permute-start.2
  22.0 5.5 collective-permute-start.3
  91.9 13.7 copy-start.40
  103.4 4.5 collective-permute-start.4
  106.6 7.7 collective-permute-start.5
  107.9 6.4 copy-start.13
  116.0 33.0 %collective-permute-start.6 = (f32[14,128,256]{2,1,0:T(8,128)}, f32[14,128,256]{2,1,0:T(8,128)}, u32[]{:S(2)}, u32[]{:S(2)}) collective-permute-start(f32[14,128,256]{2,1,0:T(8,128)} %get-tuple-element.864), channel_id=1, source_target_pairs={{0,1},{1,2},{2,3},{3,4},{4,5},{5,6},{6,7},{7,8},{8,9},{9,10},{10,1... | collective-permute-start | bytes 5505032 | tf_op jit(solution)/shard_map/ppermute | solution.py:28
  118.5 36.3 %collective-permute-start.7 = (f32[14,128,256]{2,1,0:T(8,128)}, f32[14,128,256]{2,1,0:T(8,128)}, u32[]{:S(2)}, u32[]{:S(2)}) collective-permute-start(f32[14,128,256]{2,1,0:T(8,128)} %get-tuple-element.863), channel_id=1, source_target_pairs={{1,0},{2,1},{3,2},{4,3},{5,4},{6,5},{7,6},{8,7},{9,8},{10,9},{11,1... | collective-permute-start | bytes 5505032 | tf_op jit(solution)/shard_map/ppermute | solution.py:28
  157.0 8.8 copy-start.14
  157.0 8.8 copy-start.21
  177.4 21.2 copy-start.18
  185.6 15.8 collective-permute-start.8
  197.3 12.1 collective-permute-start.9
  209.5 89.0 %collective-permute-start.10 = (f32[14,128,256]{2,1,0:T(8,128)S(1)}, f32[14,128,256]{2,1,0:T(8,128)S(1)}, u32[]{:S(2)}, u32[]{:S(2)}) collective-permute-start(f32[14,128,256]{2,1,0:T(8,128)S(1)} %get-tuple-element.856), channel_id=1, source_target_pairs={{0,1},{1,2},{2,3},{3,4},{4,5},{5,6},{6,7},{7,8},{8,9},{9,10},{10,1... | collective-permute-start | bytes 5505032 | tf_op jit(solution)/shard_map/ppermute | solution.py:28
  268.1 36.1 %collective-permute-start.11 = (f32[14,128,256]{2,1,0:T(8,128)S(1)}, f32[14,128,256]{2,1,0:T(8,128)S(1)}, u32[]{:S(2)}, u32[]{:S(2)}) collective-permute-start(f32[14,128,256]{2,1,0:T(8,128)S(1)} %get-tuple-element.855), channel_id=1, source_target_pairs={{1,0},{2,1},{3,2},{4,3},{5,4},{6,5},{7,6},{8,7},{9,8},{10,9},{11,1... | collective-permute-start | bytes 5505032 | tf_op jit(solution)/shard_map/ppermute | solution.py:28
  343.4 74.6 %collective-permute-start.12 = (f32[6,128,256]{2,1,0:T(8,128)S(1)}, f32[6,128,256]{2,1,0:T(8,128)S(1)}, u32[]{:S(2)}, u32[]{:S(2)}) collective-permute-start(f32[6,128,256]{2,1,0:T(8,128)S(1)} %get-tuple-element.944), channel_id=1, source_target_pairs={{0,16},{16,32},{32,48},{48,64},{64,80},{80,96},{96,112},{1,17},{17... | collective-permute-start | bytes 2359304 | tf_op jit(solution)/shard_map/ppermute | solution.py:28
  414.8 10.9 copy-start.97
  414.8 13.0 copy-start.51
  416.7 4.2 collective-permute-start.13
  422.6 116.1 %collective-permute-start.14 = (f32[14,128,256]{2,1,0:T(8,128)}, f32[14,128,256]{2,1,0:T(8,128)}, u32[]{:S(2)}, u32[]{:S(2)}) collective-permute-start(f32[14,128,256]{2,1,0:T(8,128)} %get-tuple-element.848), channel_id=1, source_target_pairs={{0,1},{1,2},{2,3},{3,4},{4,5},{5,6},{6,7},{7,8},{8,9},{9,10},{10,1... | collective-permute-start | bytes 5505032 | tf_op jit(solution)/shard_map/ppermute | solution.py:28
  426.5 114.4 %collective-permute-start.15 = (f32[14,128,256]{2,1,0:T(8,128)}, f32[14,128,256]{2,1,0:T(8,128)}, u32[]{:S(2)}, u32[]{:S(2)}) collective-permute-start(f32[14,128,256]{2,1,0:T(8,128)} %get-tuple-element.847), channel_id=1, source_target_pairs={{1,0},{2,1},{3,2},{4,3},{5,4},{6,5},{7,6},{8,7},{9,8},{10,9},{11,1... | collective-permute-start | bytes 5505032 | tf_op jit(solution)/shard_map/ppermute | solution.py:28
  561.0 6.9 copy-start.22
  586.0 5.9 copy-start.42
  586.7 7.2 copy-start.98
  586.7 7.2 copy-start.99
  589.8 4.7 collective-permute-start.16
  592.0 4.2 collective-permute-start.17
  597.6 82.1 %collective-permute-start.18 = (f32[14,128,256]{2,1,0:T(8,128)}, f32[14,128,256]{2,1,0:T(8,128)}, u32[]{:S(2)}, u32[]{:S(2)}) collective-permute-start(f32[14,128,256]{2,1,0:T(8,128)} %get-tuple-element.840), channel_id=1, source_target_pairs={{0,1},{1,2},{2,3},{3,4},{4,5},{5,6},{6,7},{7,8},{8,9},{9,10},{10,1... | collective-permute-start | bytes 5505032 | tf_op jit(solution)/shard_map/ppermute | solution.py:28
  652.4 36.5 %collective-permute-start.19 = (f32[14,128,256]{2,1,0:T(8,128)S(1)}, f32[14,128,256]{2,1,0:T(8,128)S(1)}, u32[]{:S(2)}, u32[]{:S(2)}) collective-permute-start(f32[14,128,256]{2,1,0:T(8,128)S(1)} %get-tuple-element.839), channel_id=1, source_target_pairs={{1,0},{2,1},{3,2},{4,3},{5,4},{6,5},{7,6},{8,7},{9,8},{10,9},{11,1... | collective-permute-start | bytes 5505032 | tf_op jit(solution)/shard_map/ppermute | solution.py:28
  680.8 9.4 copy-start.49
  680.8 9.4 copy-start.43
  680.8 9.4 copy-start.46
  680.8 9.5 copy-start.60
  680.8 9.5 copy-start.54
  680.9 10.4 copy-start.38
  680.9 10.4 copy-start.57
  716.9 6.2 copy-start.83
  716.9 8.0 copy-start.82
  716.9 8.0 copy-start.81
  717.1 7.9 copy-start.80
  744.8 22.7 copy-start.69
  746.7 39.7 %all-to-all-start = ((f32[128,9,128]{2,1,0:T(8,128)}), f32[128,9,128]{2,1,0:T(8,128)S(1)}, u32[]{:S(2)}, u32[]{:S(2)}) async-start(f32[128,9,128]{2,1,0:T(8,128)} %copy.271), calls=%async_computation | async-start | bytes 2097152 | tf_op jit(solution)/shard_map/all_to_all | solution.py:205
  767.4 427.0 %all-gather.15.cloned.1.call-start = ((), (), s32[]{:S(2)}) async-start(), calls=%async_computation.1 | async-start | bytes 71303168 | tf_op jit(solution)/shard_map/all_gather | solution.py:33
  792.0 5.4 copy-start.88
  792.0 5.4 copy-start.89
  792.0 5.4 copy-start.90
  792.0 5.4 copy-start.91
  792.0 5.4 copy-start.92
  792.0 5.4 copy-start.93
  792.0 5.4 copy-start.94
  792.0 5.4 copy-start.95
  797.4 21.9 copy-start.96
  830.5 439.2 %all-gather.17.cloned.1.call-start = ((), (), s32[]{:S(2)}) async-start(), calls=%async_computation.2 | async-start | bytes 9437184 | tf_op jit(solution)/shard_map/all_gather | solution.py:33
  1220.0 305.7 %all-gather.19.cloned.1.call-start = ((), (), s32[]{:S(2)}) async-start(), calls=%async_computation.3 | async-start | bytes 18874368 | tf_op jit(solution)/shard_map/all_gather | solution.py:33
  1372.1 41.6 %copy-start.32 = (f32[512,512]{1,0:T(8,128)}, f32[512,512]{1,0:T(8,128)S(1)}, u32[]{:S(2)}) copy-start(f32[512,512]{1,0:T(8,128)S(1)} %get-tuple-element.1240) | copy-start | bytes 3145732
  1440.4 485.1 %all-gather.21.cloned.1.call-start = ((), (), s32[]{:S(2)}) async-start(), calls=%async_computation.4 | async-start | bytes 71303168 | tf_op jit(solution)/shard_map/all_gather | solution.py:33
  1556.5 444.2 %all-gather.23.cloned.1.call-start = ((), (), s32[]{:S(2)}) async-start(), calls=%async_computation.5 | async-start | bytes 9437184 | tf_op jit(solution)/shard_map/all_gather | solution.py:33
  1950.9 305.2 %all-gather.25.cloned.1.call-start = ((), (), s32[]{:S(2)}) async-start(), calls=%async_computation.6 | async-start | bytes 18874368 | tf_op jit(solution)/shard_map/all_gather | solution.py:33
  2102.6 41.6 %copy-start.33 = (f32[512,512]{1,0:T(8,128)}, f32[512,512]{1,0:T(8,128)S(1)}, u32[]{:S(2)}) copy-start(f32[512,512]{1,0:T(8,128)S(1)} %get-tuple-element.1241) | copy-start | bytes 3145732
  2264.3 16.8 copy-start.10
  2283.3 9.0 copy-start.1
  (60 other events, 138.5 us)
Sparse Core Ops, SparseCore 0:
  830.6 363.7 all-gather.14
  1220.1 49.5 all-gather.16
  1440.5 85.1 all-gather.18
  1556.6 368.8 all-gather.20
  1951.0 49.5 all-gather.22
  2171.0 85.1 all-gather.24
